TPU v7x, 512 devices: a whole 4x8x8 slice. The times are simulated.
512 devices in a mesh: graph: 16 (over y, z_lo), gr: 4 (over z_hi), gc: 8 (over x, core).
Axes of the slice: x: 4, y: 8, z: 8 (z_hi: 4, z_lo: 2; z = z_hi * 2 + z_lo), core: 2. Of those that a mesh axis runs over, the one named last changes fastest.
Arguments:
- x_in: bfloat16 [8192, 256], P(('graph', 'gr', 'gc')), parts along dimension 0, may hold values from -64 to 64
- node_type: int32 [8192], P(('graph', 'gr', 'gc')), parts along dimension 0, may hold values from 0 to 7
- node_mask: int32 [8192], P(('graph', 'gr', 'gc')), parts along dimension 0, may hold values 0 or 1
- adj_cat: int32 [8192, 512], P(('graph', 'gc'), 'gr'), parts along dimension 0, may hold values from 0 to 4
- ori_cat: int32 [8192, 512], P(('graph', 'gc'), 'gr'), parts along dimension 0, may hold values from 0 to 7
- type_table: float32 [8, 256], replicated, may hold values from -6 to 6
- adj_table: float32 [5, 32], replicated, may hold values from -6 to 6
- ori_table: float32 [8, 32], replicated, may hold values from -6 to 6
- w_qkv: bfloat16 [256, 768], replicated, may hold values from -1.5 to 1.5
- w_film: bfloat16 [32, 512], replicated, may hold values from -0.75 to 0.75
- w_edge_out: bfloat16 [256, 32], replicated, may hold values from -0.375 to 0.375
- w_node_out: bfloat16 [256, 256], replicated, may hold values from -0.375 to 0.375
- w_node_up: bfloat16 [256, 512], replicated, may hold values from -0.375 to 0.375
- w_node_down: bfloat16 [512, 256], replicated, may hold values from -0.25 to 0.25
- w_edge_up: bfloat16 [32, 128], replicated, may hold values from -1 to 1
- w_edge_down: bfloat16 [128, 32], replicated, may hold values from -0.5 to 0.5
- node_gain1: float32 [256], replicated, may hold values from 0.25 to 1.75
- node_gain2: float32 [256], replicated, may hold values from 0.25 to 1.75
- edge_gain1: float32 [32], replicated, may hold values from 0.25 to 1.75
- edge_gain2: float32 [32], replicated, may hold values from 0.25 to 1.75
Outputs:
- node_out: bfloat16 [8192, 256], P(('graph', 'gr', 'gc')), parts along dimension 0
- edge_out: bfloat16 [32, 8192, 512], P(None, ('graph', 'gc'), 'gr'), parts along dimension 1
There are 16 independent parts, one for each index of `graph`. A program takes and returns all parts, laid end to end along the dimension named above; an argument that names none is the same for every part. Nothing has to cross between parts.
All inputs are finite; a program needn't handle non-finite values. No bound on the sum of `node_mask` on one device may be relied on, other than what follows from the above.
Results may differ from a plain program's by a relative error of at most 0.0075.
The roundings to bfloat16 on the way count: a program that leaves them out, or rounds other values in their place, can miss the bound.
Values may be sent and summed in bfloat16 or wider, within the bound.
A program may use at most 64 MiB of HBM per device.

v0:
```python
import math

import jax
import jax.numpy as jnp
from jax import lax
from jax.sharding import PartitionSpec as P

HEAD_DIM = 32


def combined_all(value, axis, join):
    pieces = jax.tree.map(lambda part: lax.all_gather(part, axis), value)
    head = jax.tree.map(lambda part: part[0], pieces)
    tail = jax.tree.map(lambda part: part[1:], pieces)
    running, _ = lax.scan(lambda running, slab: (join(running, slab), None), head, tail)
    return running


def layer_norm(values, gain, axis):
    center = values - jnp.mean(values, axis=axis, keepdims=True)
    spread = jnp.mean(center * center, axis=axis, keepdims=True)
    return center / jnp.sqrt(spread + 1e-05) * gain


def combine_stats(earlier, later):
    peak = jnp.maximum(earlier[0], later[0])
    first_factor = jnp.exp(earlier[0] - peak)
    second_factor = jnp.exp(later[0] - peak)
    return (
        peak,
        earlier[1] * first_factor + later[1] * second_factor,
        earlier[2] * first_factor + later[2] * second_factor,
    )


def category_sum(codes, lookup):
    levels = jnp.arange(lookup.shape[0], dtype=jnp.int32)
    onehot = (codes[None] == levels[:, None, None]).astype(jnp.float32)
    return jnp.einsum("acr,af->fcr", onehot, lookup, precision=lax.Precision.HIGHEST)


def body(
    x_in,
    node_type,
    node_mask,
    adj_cat,
    ori_cat,
    type_table,
    adj_table,
    ori_table,
    w_qkv,
    w_film,
    w_edge_out,
    w_node_out,
    w_node_up,
    w_node_down,
    w_edge_up,
    w_edge_down,
    node_gain1,
    node_gain2,
    edge_gain1,
    edge_gain2,
):
    width = w_node_out.shape[0]
    owned = x_in.shape[0]
    col_count, row_count = adj_cat.shape
    column_index = lax.axis_index("gc")
    type_levels = jnp.arange(type_table.shape[0], dtype=jnp.int32)
    type_onehot = (node_type[:, None] == type_levels[None, :]).astype(jnp.float32)
    embedded = jnp.dot(type_onehot, type_table, precision=lax.Precision.HIGHEST)
    nodes0 = (x_in.astype(jnp.float32) + embedded).astype(jnp.bfloat16)
    projected = jnp.dot(nodes0, w_qkv, preferred_element_type=jnp.float32).astype(jnp.bfloat16)
    query_own = projected[:, :width]
    key_own = projected[:, width : 2 * width]
    value_own = projected[:, 2 * width :]
    valid_own = node_mask.astype(jnp.bfloat16)
    query_rows, valid_rows = (
        lax.all_gather(query_own, "gc", axis=0, tiled=True),
        lax.all_gather(valid_own, "gc", axis=0, tiled=True),
    )
    key_all, value_all, valid_all = (
        lax.all_gather(key_own, ("gr", "gc"), axis=0, tiled=True),
        lax.all_gather(value_own, ("gr", "gc"), axis=0, tiled=True),
        lax.all_gather(valid_own, ("gr", "gc"), axis=0, tiled=True),
    )
    first_col = column_index * col_count
    key_cols = lax.dynamic_slice_in_dim(key_all, first_col, col_count, 0)
    value_cols = lax.dynamic_slice_in_dim(value_all, first_col, col_count, 0)
    valid_cols = lax.dynamic_slice_in_dim(valid_all, first_col, col_count, 0)
    edges0 = (category_sum(adj_cat, adj_table) + category_sum(ori_cat, ori_table)).astype(
        jnp.bfloat16
    )
    edge_width = edges0.shape[0]
    score_scale = 1.0 / math.sqrt(HEAD_DIM)
    query_t = query_rows.astype(jnp.float32).T
    key_block = min(16, col_count)
    turns = col_count // key_block

    def sweep(turn, state):
        peak, summed, weighted, messages = state
        begin_at = turn * key_block
        edge_part = lax.dynamic_slice_in_dim(edges0, begin_at, key_block, 1)
        film = jnp.einsum("fjr,fk->kjr", edge_part, w_film, preferred_element_type=jnp.float32)
        key_part = lax.dynamic_slice_in_dim(key_cols, begin_at, key_block, 0).astype(jnp.float32).T
        value_part = (
            lax.dynamic_slice_in_dim(value_cols, begin_at, key_block, 0).astype(jnp.float32).T
        )
        valid_part = lax.dynamic_slice_in_dim(valid_cols, begin_at, key_block, 0)
        scores = (
            key_part[:, :, None] * query_t[:, None, :] * score_scale * (film[:width] + 1.0)
            + film[width:]
        )
        message = jnp.einsum(
            "cjr,cf->fjr",
            scores.astype(jnp.bfloat16),
            w_edge_out,
            preferred_element_type=jnp.float32,
        )
        masked = jnp.where(valid_part[None, :, None] > 0, scores, -1000000000.0)
        new_peak = jnp.maximum(peak, jnp.max(masked, axis=1))
        factor = jnp.exp(peak - new_peak)
        expo = jnp.exp(masked - new_peak[:, None, :])
        summed = summed * factor + jnp.sum(expo, axis=1)
        weighted = weighted * factor + jnp.sum(expo * value_part[:, :, None], axis=1)
        messages = lax.dynamic_update_slice_in_dim(messages, message, begin_at, 1)
        return (new_peak, summed, weighted, messages)

    initial = (
        jnp.full((width, row_count), -1e30, jnp.float32),
        jnp.zeros((width, row_count), jnp.float32),
        jnp.zeros((width, row_count), jnp.float32),
        jnp.zeros((edge_width, col_count, row_count), jnp.float32),
    )
    peak, summed, weighted, messages = lax.fori_loop(0, turns, sweep, initial)
    peak, summed, weighted = combined_all((peak, summed, weighted), "gc", combine_stats)
    attended = lax.dynamic_slice_in_dim(weighted / summed, column_index * owned, owned, 1).T
    valid_node = valid_own.astype(jnp.float32)
    attn_bf = attended.astype(jnp.bfloat16)
    nodes1 = layer_norm(
        nodes0.astype(jnp.float32)
        + jnp.dot(attn_bf, w_node_out, preferred_element_type=jnp.float32),
        node_gain1,
        -1,
    ).astype(jnp.bfloat16)
    hidden_node = jnp.maximum(
        jnp.dot(nodes1, w_node_up, preferred_element_type=jnp.float32), 0.0
    ).astype(jnp.bfloat16)
    node_out = (
        layer_norm(
            nodes1.astype(jnp.float32)
            + jnp.dot(hidden_node, w_node_down, preferred_element_type=jnp.float32),
            node_gain2,
            -1,
        )
        * valid_node[:, None]
    ).astype(jnp.bfloat16)
    edges1 = layer_norm(edges0.astype(jnp.float32) + messages, edge_gain1[:, None, None], 0).astype(
        jnp.bfloat16
    )
    hidden_edge = jnp.maximum(
        jnp.einsum("fjr,fh->hjr", edges1, w_edge_up, preferred_element_type=jnp.float32), 0.0
    ).astype(jnp.bfloat16)
    edges2 = layer_norm(
        edges1.astype(jnp.float32)
        + jnp.einsum("hjr,hf->fjr", hidden_edge, w_edge_down, preferred_element_type=jnp.float32),
        edge_gain2[:, None, None],
        0,
    )
    edge_out = (
        edges2
        * valid_cols.astype(jnp.float32)[None, :, None]
        * valid_rows.astype(jnp.float32)[None, None, :]
    ).astype(jnp.bfloat16)
    return (node_out, edge_out)


def solution(mesh):
    return jax.shard_map(
        body,
        mesh=mesh,
        in_specs=(
            P(("graph", "gr", "gc"), None),
            P(("graph", "gr", "gc")),
            P(("graph", "gr", "gc")),
            P(("graph", "gc"), "gr"),
            P(("graph", "gc"), "gr"),
            P(),
            P(),
            P(),
            P(),
            P(),
            P(),
            P(),
            P(),
            P(),
            P(),
            P(),
            P(),
            P(),
            P(),
            P(),
        ),
        out_specs=(P(("graph", "gr", "gc"), None), P(None, ("graph", "gc"), "gr")),
        check_vma=False,
    )
```

profile of v0, /device:TPU:1, one launch (start us, length us, event | category | flops | bytes accessed | tf_op | source)
XLA Modules:
  0.0 318.0 jit_solution(9639753481749543636)
XLA Ops:
  7.3 1.2 convert_convert_fusion
  8.5 1.3 dynamic-slice
  10.7 76.1 %all-reduce = bf16[512]{0:T(512)(128)(2,1)S(1)} all-reduce(bf16[512]{0:T(512)(128)(2,1)S(1)} %dynamic-update-slice), channel_id=1, replica_groups=mesh['graph'=16,'gr'=4,'gc'=8] {'gr','gc'}, use_global_device_ids=true, to_apply=%add | all-reduce | flops 512 | bytes 2048
  88.3 45.3 %all_gather.36 = bf16[512,256]{1,0:T(8,128)(2,1)S(1)} all-gather(bf16[16,256]{1,0:T(8,128)(2,1)S(1)} %get-tuple-element.348), channel_id=1, replica_groups=mesh['graph'=16,'gr'=4,'gc'=8] {'gr','gc'}, dimensions={0}, use_global_device_ids=true | all-gather | bytes 270336 | tf_op jit(solution)/shard_map/all_gather | solution.py:83
  134.9 41.5 %all_gather.34 = bf16[512,256]{1,0:T(8,128)(2,1)S(1)} all-gather(bf16[16,256]{1,0:T(8,128)(2,1)S(1)} %get-tuple-element.350), channel_id=1, replica_groups=mesh['graph'=16,'gr'=4,'gc'=8] {'gr','gc'}, dimensions={0}, use_global_device_ids=true | all-gather | bytes 270336 | tf_op jit(solution)/shard_map/all_gather | solution.py:82
  177.0 12.7 %all_gather.35 = bf16[128,256]{1,0:T(8,128)(2,1)S(1)} all-gather(bf16[16,256]{1,0:T(8,128)(2,1)S(1)} %get-tuple-element.349), channel_id=1, replica_groups=mesh['graph'=16,'gr'=4,'gc'=8] {'gc'}, dimensions={0}, use_global_device_ids=true | all-gather | bytes 73728 | tf_op jit(solution)/shard_map/all_gather | solution.py:78
  190.4 1.4 fusion.32
  192.4 1.1 broadcast_in_dim.67
  193.5 24.5 %while.35 = (s32[]{:T(128)}, f32[256,128]{0,1:T(8,128)S(1)}, f32[256,128]{0,1:T(8,128)S(1)}, f32[256,128]{0,1:T(8,128)S(1)}, f32[32,64,128]{2,0,1:T(8,128)}, /*i...) while((s32[]{:T(128)}, f32[256,128]{0,1:T(8,128)S(1)}, ...), condition=%wide.region_4.5_spmd.clone, body=%wide.region_0.4_spmd.clone.sunk | while | flops 107716664 | bytes 18153920 | solution.py:134
  194.3 1.5 convolution_bitcast_fusion.3
  197.2 1.1 fusion.81
  198.3 1.2 multiply_reduce_fusion.6
  200.4 1.5 convolution_bitcast_fusion.3
  204.5 1.2 multiply_reduce_fusion.6
  206.5 1.5 convolution_bitcast_fusion.3
  209.5 1.1 fusion.81
  210.6 1.2 multiply_reduce_fusion.6
  212.7 1.5 convolution_bitcast_fusion.3
  216.7 1.2 multiply_reduce_fusion.6
  220.6 1.5 fusion.31
  222.0 1.3 dynamic-slice.1
  224.2 11.9 %all-reduce.1 = bf16[128]{0:T(256)(128)(2,1)S(1)} all-reduce(bf16[128]{0:T(256)(128)(2,1)S(1)} %dynamic-update-slice.1), channel_id=1, replica_groups=mesh['graph'=16,'gr'=4,'gc'=8] {'gc'}, use_global_device_ids=true, to_apply=%add.1 | all-reduce | flops 128 | bytes 512
  236.2 1.5 multiply_reduce_fusion.2
  237.8 2.6 fusion.57
  243.1 1.2 slice.66
  244.3 29.6 %all-gather.9.cloned.1.call-done = f32[2048,128]{1,0:T(8,128)} async-done(((f32[256,128]{1,0:T(8,128)}), f32[2048,128]{1,0:T(8,128)}) %all-gather.9.cloned.1.call-update) | async-done | bytes 1048592 | tf_op jit(solution)/shard_map/all_gather | solution.py:12
  273.9 1.3 slice.67
  275.2 29.4 %all-gather.11.cloned.1.call-done = f32[2048,128]{1,0:T(8,128)} async-done(((f32[256,128]{1,0:T(8,128)}), f32[2048,128]{1,0:T(8,128)}) %all-gather.11.cloned.1.call-update) | async-done | bytes 1048592 | tf_op jit(solution)/shard_map/all_gather | solution.py:12
  304.6 1.3 slice.68
  305.9 1.6 while.34
  307.6 1.3 fusion.55
  309.1 1.5 fusion.56
  (145 shorter events, 24.1 us)
Async XLA Ops:
  7.2 80.6 %copy-start = (bf16[256,768]{1,0:T(8,128)(2,1)S(1)}, bf16[256,768]{1,0:T(8,128)(2,1)}, u32[]{:S(2)}) copy-start(bf16[256,768]{1,0:T(8,128)(2,1)} %param.32) | copy-start | bytes 1179652
  7.2 184.6 %copy-start.4 = (s32[64,128]{1,0:T(8,128)S(1)}, s32[64,128]{1,0:T(8,128)}, u32[]{:S(2)}) copy-start(s32[64,128]{1,0:T(8,128)} %param.28) | copy-start | bytes 98308
  7.2 184.6 %copy-start.7 = (f32[8,32]{1,0:T(8,128)S(1)}, f32[8,32]{1,0:T(8,128)}, u32[]{:S(2)}) copy-start(f32[8,32]{1,0:T(8,128)} %param.31) | copy-start | bytes 3076
  7.2 235.9 %all-gather.7.cloned.1.call-start = ((), (), s32[]{:S(2)}) async-start(), calls=%async_computation | async-start | bytes 1179648 | tf_op jit(solution)/shard_map/all_gather | solution.py:12
  8.5 78.3 %copy-start.15 = (bf16[16]{0:T(256)(128)(2,1)}, bf16[16]{0:T(256)(128)(2,1)S(1)}, u32[]{:S(2)}) copy-start(bf16[16]{0:T(256)(128)(2,1)S(1)} %get-tuple-element.352) | copy-start | bytes 100
  87.7 0.6 copy-start.5
  194.3 2.2 copy-start.1
  196.5 0.5 copy-start.3
  196.5 0.7 copy-start.2
  200.4 2.2 copy-start.1
  202.6 0.5 copy-start.3
  202.6 0.7 copy-start.2
  206.5 2.2 copy-start.1
  208.7 0.5 copy-start.3
  208.7 0.7 copy-start.2
  212.7 2.2 copy-start.1
  214.9 0.5 copy-start.3
  214.9 0.7 copy-start.2
  218.1 5.9 %copy-start.16 = (bf16[16]{0:T(256)(128)(2,1)S(1)}, bf16[16]{0:T(256)(128)(2,1)}, u32[]{:S(2)}) copy-start(bf16[16]{0:T(256)(128)(2,1)} %copy-done.15) | copy-start | bytes 100
  218.9 18.9 %copy-start.12 = (bf16[32,128]{1,0:T(8,128)(2,1)S(1)}, bf16[32,128]{1,0:T(8,128)(2,1)}, u32[]{:S(2)}) copy-start(bf16[32,128]{1,0:T(8,128)(2,1)} %param.38) | copy-start | bytes 24580
  218.9 18.9 %copy-start.13 = (bf16[128,32]{0,1:T(8,128)(2,1)S(1)}, bf16[128,32]{0,1:T(8,128)(2,1)}, u32[]{:S(2)}) copy-start(bf16[128,32]{0,1:T(8,128)(2,1)} %param.39) | copy-start | bytes 24580
  218.9 18.9 %copy-start.14 = (f32[32]{0:T(128)S(1)}, f32[32]{0:T(128)}, u32[]{:S(2)}) copy-start(f32[32]{0:T(128)} %param.42) | copy-start | bytes 388
  218.9 55.0 %all-gather.9.cloned.1.call-start = ((), (), s32[]{:S(2)}) async-start(), calls=%async_computation.1 | async-start | bytes 1179648 | tf_op jit(solution)/shard_map/all_gather | solution.py:12
  219.7 84.9 %all-gather.11.cloned.1.call-start = ((), (), s32[]{:S(2)}) async-start(), calls=%async_computation.2 | async-start | bytes 1179648 | tf_op jit(solution)/shard_map/all_gather | solution.py:12
  237.8 2.9 copy-start.8
  237.8 2.9 copy-start.10
  244.3 61.5 %slice-start = ((f32[2048,128]{1,0:T(8,128)}), f32[256,128]{1,0:T(8,128)S(1)}, s32[]{:S(2)}) async-start(f32[2048,128]{1,0:T(8,128)} %all-gather.7.cloned.1.call-done), calls=%async_computation.3 | async-start | bytes 262144 | tf_op jit(solution)/shard_map/slice | solution.py:13
  273.9 32.0 %slice-start.1 = ((f32[2048,128]{1,0:T(8,128)}), f32[256,128]{1,0:T(8,128)S(1)}, s32[]{:S(2)}) async-start(f32[2048,128]{1,0:T(8,128)} %all-gather.9.cloned.1.call-done), calls=%async_computation.4 | async-start | bytes 262144 | tf_op jit(solution)/shard_map/slice | solution.py:13
  304.6 1.3 slice-start.2
  305.9 1.7 copy-start.6
  305.9 4.9 %copy-start.9 = (f32[256]{0:T(256)S(1)}, f32[256]{0:T(256)}, u32[]{:S(2)}) copy-start(f32[256]{0:T(256)} %param.41) | copy-start | bytes 3076
  305.9 4.9 %copy-start.11 = (f32[16]{0:T(128)S(1)}, f32[16]{0:T(128)}, u32[]{:S(2)}) copy-start(f32[16]{0:T(128)} %get-tuple-element.351) | copy-start | bytes 196
Sparse Core Ops, SparseCore 0:
  219.0 24.0 all-gather.6
  245.2 28.6 all-gather.8
  276.1 28.4 all-gather.10
where the time goes:
time: 319 us; the launch traced here: 318 us
  blocking collectives  188 us (59%)
  waiting for transfers between devices  60.1 us (19%)
  other arithmetic  21.5 us (7%)
  matrix products  19.1 us (6%)
  between operations  15.5 us (5%)
  local copies, waits for them, and re-layouts  13.8 us (4%)
    unnamed x2, blocking collectives  88.1 us
    all_gather x3, waiting for transfers between devices, combined_all(): pieces = jax.tree.map(lambda part: lax.all_gather(part, axis), value)  60 us
    all_gather x1, blocking collectives, body(): lax.all_gather(value_own, ('gr', 'gc'), axis=0, tiled=True)  45.3 us
    all_gather x1, blocking collectives, body(): lax.all_gather(key_own, ('gr', 'gc'), axis=0, tiled=True)  41.5 us
    all_gather x1, blocking collectives, body(): lax.all_gather(query_own, 'gc', axis=0, tiled=True)  12.7 us
  transfers between devices with their start and end apart: 3, of which 3 were waited for; matrix products, arithmetic and copies ran while one was open for 4% of the time, Pallas kernels for 0%

commit v1 on v0

v1 whole, which is shorter than its diff:
```python
import functools
import math

import jax
import jax.numpy as jnp
from jax import lax
from jax.experimental import pallas as pl
from jax.experimental.pallas import tpu as pltpu
from jax.sharding import PartitionSpec as P

MESH = pl.DeviceIdType.MESH
F32, BF16 = jnp.float32, jnp.bfloat16
HEAD_DIM = 32
LOG2E = math.log2(math.e)
NEG = -1000000000.0
NT = (((1,), (1,)), ((), ()))


def dot(a, b):
    return jnp.dot(a, b, preferred_element_type=F32)


def dot_nt(a, b):
    return lax.dot_general(a, b, NT, preferred_element_type=F32)


def eye(n):
    rows = lax.broadcasted_iota(jnp.int32, (n, n), 0)
    cols = lax.broadcasted_iota(jnp.int32, (n, n), 1)
    return rows == cols


def norm(u, axis):
    center = u - jnp.mean(u, axis=axis, keepdims=True)
    spread = jnp.mean(center * center, axis=axis, keepdims=True)
    return center / jnp.sqrt(spread + 1e-05)


def kernel(
    x_h, type_s, mask_s, adj_h, ori_h, ttab_h, atab_h, otab_h, wqkv_h, wfilm_h,
    weo_h, wno_h, wnu_h, wnd_h, weu_h, wed_h, ng1_h, ng2_h, eg1_h, eg2_h,
    node_o, edge_o,
    x_v, adj_v, ori_v, ttab_v, atab_v, otab_v, wqkv_v, wfilm_v,
    weo_v, wno_v, wnu_v, wnd_v, weu_v, wed_v, ng1_v, ng2_v, eg1_v, eg2_v,
    node_v, edge_v,
    send, xq, xk, stat, rstat,
    t40, ft32, ftab, t40t, codes, onehot, film, score, e0, yrow,
    q_v, k_v, v_v, km_v, weot, weut, wedt, g1c, g2c,
    in_sem, out_sem, sendq, recvq, sendk, recvk, sends, recvs,
):
    gr, gc = lax.axis_index("gr"), lax.axis_index("gc")
    n_gr, n_gc = 4, 8

    pairs = [
        (x_h, x_v), (ttab_h, ttab_v), (adj_h, adj_v), (ori_h, ori_v),
        (atab_h, atab_v), (otab_h, otab_v), (wfilm_h, wfilm_v), (wqkv_h, wqkv_v),
        (weo_h, weo_v), (weu_h, weu_v), (wed_h, wed_v), (eg1_h, eg1_v), (eg2_h, eg2_v),
        (wno_h, wno_v), (wnu_h, wnu_v), (wnd_h, wnd_v), (ng1_h, ng1_v), (ng2_h, ng2_v),
    ]
    loads = [pltpu.make_async_copy(a, b, in_sem.at[i]) for i, (a, b) in enumerate(pairs)]

    barrier = pltpu.get_barrier_semaphore()
    far = lax.div(gc, 2) != gr
    for t in range(1, n_gc):
        pl.semaphore_signal(
            barrier, inc=1, device_id={"gc": lax.rem(gc + t, n_gc)}, device_id_type=MESH
        )

    @pl.when(far)
    def _():
        for t in range(4):
            pl.semaphore_signal(
                barrier, inc=1,
                device_id={"gr": lax.div(gc, 2), "gc": 4 * lax.rem(gc, 2) + t},
                device_id_type=MESH,
            )

    for copy in loads:
        copy.start()

    loads[0].wait()
    loads[1].wait()
    row_id = lax.broadcasted_iota(jnp.int32, (16, 256), 0)
    embedded = jnp.zeros((16, 256), F32)
    valid = jnp.zeros((16, 128), F32)
    for r in range(16):
        line = ttab_v[pl.ds(type_s[r], 1), :]
        embedded = jnp.where(row_id == r, line, embedded)
        valid = jnp.where(row_id[:, :128] == r, mask_s[r].astype(F32), valid)
    send[:, :256] = (x_v[...].astype(F32) + embedded).astype(BF16)
    send[:, 256:] = valid.astype(BF16)
    xq[pl.ds(gc, 1)] = send[...][None]

    def q_copy(peer, slot, index):
        return pltpu.make_async_remote_copy(
            src_ref=send, dst_ref=xq.at[slot], send_sem=sendq.at[index],
            recv_sem=recvq.at[slot], device_id={"gc": peer}, device_id_type=MESH,
        )

    def k_copy(peer, slot, index):
        return pltpu.make_async_remote_copy(
            src_ref=send, dst_ref=xk.at[slot], send_sem=sendk.at[index],
            recv_sem=recvk.at[slot],
            device_id={"gr": peer, "gc": 2 * gr + lax.div(gc, 4)}, device_id_type=MESH,
        )

    pl.semaphore_wait(barrier, n_gc - 1 + n_gr - 1)
    k_sent = [k_copy(lax.rem(gr + t, n_gr), lax.rem(gc, 4), t - 1) for t in (2, 1, 3)]
    q_sent = [q_copy(lax.rem(gc + t, n_gc), gc, t - 1) for t in (4, 3, 5, 2, 6, 1, 7)]
    for copy in k_sent + q_sent:
        copy.start()

    loads[4].wait()
    loads[5].wait()
    loads[6].wait()
    t40[...] = jnp.zeros_like(t40)
    ft32[...] = jnp.zeros_like(ft32)
    for a in range(5):
        t40[8 * a : 8 * a + 8, :32] = atab_v[a : a + 1, :] + otab_v[...]
    table = t40[...].astype(BF16)
    values = dot(table[:40, :32], wfilm_v[...])
    lane = lax.broadcasted_iota(jnp.int32, (40, 512), 1)
    values = values + jnp.where(lane < 256, 1.0, 0.0)
    high = values.astype(BF16).astype(F32)
    middle = (values - high).astype(BF16).astype(F32)
    ft32[0:40] = high
    ft32[40:80] = middle
    ft32[80:120] = values - high - middle
    ftab[...] = ft32[...].astype(BF16)
    t40t[...] = t40[...].T[:32].astype(BF16)

    loads[2].wait()
    loads[3].wait()
    code = (adj_v[...] * 8 + ori_v[...]).astype(F32)
    code_t = jnp.concatenate([code, code], axis=0).T
    for b in range(8):
        codes[b] = pltpu.roll(code_t, (128 - 8 * b) % 128, 1)
    lane = lax.broadcasted_iota(jnp.int32, (128, 128), 1)
    label = jnp.where(lane < 40, lane, jnp.where(lane < 80, lane - 40, lane - 80))
    label = jnp.where(lane < 120, label, -1).astype(F32)

    def film_block(b, carry):
        block = codes[b]
        for r in range(8):
            hit = jnp.broadcast_to(block[:, r : r + 1], (128, 128)) == label
            onehot[128 * r : 128 * r + 128] = jnp.where(hit, 1.0, 0.0).astype(BF16)
        hot = onehot[...]
        film[pl.ds(b * 8, 8)] = dot(hot, ftab[...]).reshape(8, 128, 512)
        e0[:, pl.ds(pl.multiple_of(b * 1024, 1024), 1024)] = dot_nt(t40t[...], hot)
        return carry

    lax.fori_loop(0, 8, film_block, 0)

    for i in range(7, 13):
        loads[i].wait()
    ident = jnp.where(eye(32), 1.0, 0.0).astype(BF16)
    weot[...] = dot_nt(ident, weo_v[...]).astype(BF16)
    wedt[...] = dot_nt(ident, wed_v[...]).astype(BF16)
    weut[...] = weu_v[...].astype(F32).T.astype(BF16)
    for g_ref, c_ref in ((eg1_v, g1c), (eg2_v, g2c)):
        spread = jnp.where(eye(32), jnp.broadcast_to(g_ref[...], (32, 32)), 0.0)
        c_ref[...] = jnp.broadcast_to(jnp.sum(spread, axis=1, keepdims=True), (32, 128))

    for t in range(1, n_gc):
        q_copy(gc, lax.rem(gc + t, n_gc), 0).wait_recv()
    nodes_q = xq[...].reshape(128, 384)
    q = dot(nodes_q[:, :256], wqkv_v[:, :256]).astype(BF16)
    q_v[...] = q.astype(F32) * (1.0 / math.sqrt(HEAD_DIM))
    row_mask = nodes_q[:, 256:].astype(F32).T[0:1, :]

    @pl.when(far)
    def _():
        for t in range(4):
            k_copy(gr, t, 0).wait_recv()

    @pl.when(jnp.logical_not(far))
    def _():
        xk[...] = xq[pl.ds(4 * lax.rem(gc, 2), 4)]

    nodes_k = xk[...].reshape(64, 384)
    kv = dot(nodes_k[:, :256], wqkv_v[:, 256:]).astype(BF16).astype(F32)
    k_v[...] = kv[:, :256]
    v_v[...] = kv[:, 256:]
    km_v[...] = nodes_k[:, 256:].astype(F32)

    def s_copy(owner, slot, index):
        return pltpu.make_async_remote_copy(
            src_ref=stat.at[owner], dst_ref=rstat.at[slot], send_sem=sends.at[index],
            recv_sem=recvs.at[slot], device_id={"gc": owner}, device_id_type=MESH,
        )

    def attend(t, carry):
        owner = lax.rem(gc + t + 1, n_gc)
        first = pl.multiple_of(owner * 16, 16)
        qs = q_v[pl.ds(first, 16), :]

        def peak_block(b, peak):
            for r in range(8):
                j = b * 8 + r
                live = jnp.broadcast_to(km_v[pl.ds(j, 1), :], (16, 128)) > 0
                live = jnp.concatenate([live, live], axis=1)
                k = jnp.broadcast_to(k_v[pl.ds(j, 1), :], (16, 256))
                s = k * qs * film[j, pl.ds(first, 16), :256] + film[j, pl.ds(first, 16), 256:]
                s = jnp.where(live, s, NEG)
                score[j, pl.ds(first, 16), :] = s
                peak = jnp.maximum(peak, s)
            return peak

        peak = lax.fori_loop(0, 8, peak_block, jnp.full((16, 256), -3e38, F32))

        def sum_block(b, state):
            total, weighted = state
            for r in range(8):
                j = b * 8 + r
                v = jnp.broadcast_to(v_v[pl.ds(j, 1), :], (16, 256))
                p = jnp.exp2((score[j, pl.ds(first, 16), :] - peak) * LOG2E)
                total = total + p
                weighted = weighted + p * v
            return total, weighted

        zero = jnp.zeros((16, 256), F32)
        total, weighted = lax.fori_loop(0, 8, sum_block, (zero, zero))
        stat[owner, 0] = peak
        stat[owner, 1] = total
        stat[owner, 2] = weighted

        @pl.when(t >= 1)
        def _():
            s_copy(lax.rem(gc + t, n_gc), gc, t - 1).start()

        return carry

    lax.fori_loop(0, n_gc, attend, 0)

    def edge_block(b, carry):
        for h in range(4):
            j = b * 16 + h * 4
            cols = pl.ds(pl.multiple_of(j * 128, 512), 512)
            sb = score[pl.ds(j, 4)].reshape(512, 256).astype(BF16)
            u = e0[:, cols] + dot_nt(weot[...], sb)
            gain = jnp.concatenate([g1c[...]] * 4, axis=1)
            e1 = (norm(u, 0) * gain).astype(BF16)
            hidden = jnp.maximum(dot(weut[...], e1), 0.0).astype(BF16)
            u = e1.astype(F32) + dot(wedt[...], hidden)
            gain = jnp.concatenate([g2c[...]] * 4, axis=1)
            y = norm(u, 0) * gain
            for r in range(4):
                yrow[pl.ds(h * 4 + r, 32, stride=16), :] = y[:, 128 * r : 128 * r + 128]
        keep = km_v[pl.ds(b * 16, 16), :] * row_mask
        edge_v[:, pl.ds(b * 16, 16), :] = (yrow[...].reshape(32, 16, 128) * keep[None]).astype(BF16)
        return carry

    lax.fori_loop(0, 4, edge_block, 0)
    out_edge = pltpu.make_async_copy(edge_v, edge_o, out_sem.at[0])
    out_edge.start()

    for i in range(13, 18):
        loads[i].wait()
    rstat[pl.ds(gc, 1)] = stat[pl.ds(gc, 1)]
    for t in range(1, n_gc):
        s_copy(gc, lax.rem(gc + t, n_gc), 0).wait_recv()
    peak = rstat[0, 0]
    for s in range(1, n_gc):
        peak = jnp.maximum(peak, rstat[s, 0])
    total = jnp.zeros((16, 256), F32)
    weighted = jnp.zeros((16, 256), F32)
    for s in range(n_gc):
        factor = jnp.exp2((rstat[s, 0] - peak) * LOG2E)
        total = total + rstat[s, 1] * factor
        weighted = weighted + rstat[s, 2] * factor
    attn = (weighted / total).astype(BF16)
    own = send[...].astype(F32)
    n1 = (norm(own[:, :256] + dot(attn, wno_v[...]), 1) * ng1_v[...]).astype(BF16)
    hid = jnp.maximum(dot(n1, wnu_v[...]), 0.0).astype(BF16)
    n2 = norm(n1.astype(F32) + dot(hid, wnd_v[...]), 1) * ng2_v[...]
    node_v[...] = (n2 * jnp.concatenate([own[:, 256:]] * 2, axis=1)).astype(BF16)
    out_node = pltpu.make_async_copy(node_v, node_o, out_sem.at[1])
    out_node.start()
    for copy in k_sent + q_sent:
        copy.wait_send()
    for t in range(n_gc - 1):
        s_copy(gc, gc, t).wait_send()
    out_edge.wait()
    out_node.wait()


def body(*args):
    (x_in, node_type, node_mask, adj, ori, ttab, atab, otab, wqkv, wfilm,
     weo, wno, wnu, wnd, weu, wed, ng1, ng2, eg1, eg2) = args
    args = (x_in, node_type, node_mask, adj, ori, ttab, atab, otab, wqkv, wfilm,
            weo, wno, wnu, wnd, weu, wed, ng1[None], ng2[None], eg1[None], eg2[None])
    anyspace = pl.BlockSpec(memory_space=pl.ANY)
    smem = pl.BlockSpec(memory_space=pltpu.SMEM)
    V = pltpu.VMEM
    D = pltpu.SemaphoreType.DMA
    loaded = [args[0]] + list(args[3:])
    return pl.pallas_call(
        kernel,
        out_shape=(
            jax.ShapeDtypeStruct((16, 256), BF16),
            jax.ShapeDtypeStruct((32, 64, 128), BF16),
        ),
        in_specs=[anyspace, smem, smem] + [anyspace] * 17,
        out_specs=(anyspace, anyspace),
        scratch_shapes=[V(a.shape, a.dtype) for a in loaded] + [
            V((16, 256), BF16),
            V((32, 64, 128), BF16),
            V((16, 384), BF16),
            V((8, 16, 384), BF16),
            V((4, 16, 384), BF16),
            V((8, 3, 16, 256), F32),
            V((8, 3, 16, 256), F32),
            V((128, 128), F32),
            V((128, 512), F32),
            V((128, 512), BF16),
            V((32, 128), BF16),
            V((8, 128, 128), F32),
            V((1024, 128), BF16),
            V((64, 128, 512), F32),
            V((64, 128, 256), F32),
            V((32, 8192), F32),
            V((512, 128), F32),
            V((128, 256), F32),
            V((64, 256), F32),
            V((64, 256), F32),
            V((64, 128), F32),
            V((32, 256), BF16),
            V((128, 32), BF16),
            V((32, 128), BF16),
            V((32, 128), F32),
            V((32, 128), F32),
            D((18,)), D((2,)), D((7,)), D((8,)), D((3,)), D((4,)), D((7,)), D((8,)),
        ],
        compiler_params=pltpu.CompilerParams(
            collective_id=0, has_side_effects=True, vmem_limit_bytes=60 * 1024 * 1024
        ),
    )(*args)


def solution(mesh):
    nodes = P(("graph", "gr", "gc"))
    rows = P(("graph", "gr", "gc"), None)
    pair = P(("graph", "gc"), "gr")
    return jax.shard_map(
        body,
        mesh=mesh,
        in_specs=(rows, nodes, nodes, pair, pair) + (P(),) * 15,
        out_specs=(rows, P(None, ("graph", "gc"), "gr")),
        check_vma=False,
    )
```

time: 319 us -> 36.8 us (0.12)
  blocking collectives: 188 us -> 0 us
  waiting for transfers between devices: 60.1 us -> 0 us
  Pallas kernels: 0 us -> 30.4 us
  other arithmetic: 21.5 us -> 0 us
  matrix products: 19.1 us -> 0 us
  between operations: 15.5 us -> 0.65 us
  local copies, waits for them, and re-layouts: 13.8 us -> 5.31 us
    all_gather x3 -> x0, blocking collectives: 99.5 us -> none  [the longest x1 45.3 us: body(): lax.all_gather(value_own, ('gr', 'gc'), axis=0, tiled=True)]
    unnamed x2 -> x0, blocking collectives: 88.1 us -> none
    all_gather x3 -> x0, waiting for transfers between devices: 60 us -> none  [combined_all(): pieces = jax.tree.map(lambda part: lax.all_gather(part, axis), value)]
    pallas_call x0 -> x1, Pallas kernels: none -> 30.4 us  [body(): pl.pallas_call(kernel, out_shape=(jax.ShapeDtypeStruct((16, 256), BF16),...]
    dot_general x15 -> x0, matrix products: 19.1 us -> none  [the longest x4 6.07 us: sweep(): jnp.einsum('fjr,fk->kjr', edge_part, w_film, preferred_element_type=jnp.f...]
    reduce_sum x9 -> x0, other arithmetic: 8.34 us -> none  [the longest x4 4.74 us: sweep(): jnp.sum(expo * value_part[:, :, None], axis=1)]
    slice x10 -> x0, local copies, waits for them, and re-layouts: 3.8 us -> none  [the longest x3 3.79 us: combined_all(): tail = jax.tree.map(lambda part: part[1:], pieces)]
    transpose x5 -> x0, other arithmetic: 3.55 us -> none  [the longest x4 2.89 us: sweep(): lax.dynamic_slice_in_dim(value_cols, begin_at, key_block, 0)]
  transfers between devices with their start and end apart: 3 -> 0, of which waited for: 3 -> 0; matrix products, arithmetic and copies ran while one was open for 4% -> 0% of each run, Pallas kernels for 0% -> 0%
where the time goes in v1:
time: 36.8 us; the launch traced here: 36.3 us
  Pallas kernels  30.4 us (83%)
  local copies, waits for them, and re-layouts  5.31 us (14%)
  between operations  0.65 us (2%)
    pallas_call x1, Pallas kernels, body(): pl.pallas_call(kernel, out_shape=(jax.ShapeDtypeStruct((16, 256), BF16),...  30.4 us
    unnamed x6, local copies, waits for them, and re-layouts  5.31 us

profile of v1, /device:TPU:1, one launch (start us, length us, event | category | flops | bytes accessed | tf_op | source)
XLA Modules:
  0.0 36.3 jit_solution(11572220531719723542)
XLA Ops:
  0.6 0.0 copy-start
  0.6 1.4 %copy.23.wed_h = bf16[128,32]{1,0:T(8,128)(2,1)} copy(bf16[128,32]{0,1:T(8,128)(2,1)} %param.35) | data formatting | bytes 16384 | tf_op args[15]
  2.0 0.0 copy-done
  2.1 0.7 %copy.22.weo_h = bf16[256,32]{1,0:T(8,128)(2,1)} copy(bf16[256,32]{0,1:T(8,128)(2,1)S(1)} %copy-done) | data formatting | bytes 32768 | tf_op args[10]
  2.8 30.4 %shard_map.203 = (bf16[16,256]{1,0:T(8,128)(2,1)}, bf16[32,64,128]{2,1,0:T(8,128)(2,1)}) custom-call(bf16[16,256]{1,0:T(8,128)(2,1)} %x_h.1, s32[16]{0:T(128)} %type_s.1, s32[16]{0:T(128)} %mask_s.1, s32[64,128]{1,0:T(8,128)} %adj_h.1, s32[64,128]{1,0:T(8,128)} %ori_h.1, f32[8,256]{1,0:T(8,128)} %ttab_h.1, f32[5,32]{1,0:T(8,128)} %atab_h.1, f32[8,32]{1,0:T(8,128)} %otab_h.1, ...), custom_call_target="tpu_custom_call" | custom-call | tf_op jit(solution)/shard_map/pallas_call | solution.py:297
  33.2 1.3 %copy.26 = bf16[16,256]{1,0:T(8,128)(2,1)} copy(bf16[16,256]{1,0:T(8,128)(2,1)} %get-tuple-element.4) | data formatting | bytes 16384
  34.4 1.9 %copy.27 = bf16[32,64,128]{2,1,0:T(8,128)(2,1)} copy(bf16[32,64,128]{2,1,0:T(8,128)(2,1)} %get-tuple-element.5) | data formatting | bytes 1048576
Async XLA Ops:
  0.6 1.4 %copy-start = (bf16[256,32]{0,1:T(8,128)(2,1)S(1)}, bf16[256,32]{0,1:T(8,128)(2,1)}, u32[]{:S(2)}) copy-start(bf16[256,32]{0,1:T(8,128)(2,1)} %param.30) | copy-start | bytes 49156

commit v2 on v1

v2 whole, which is shorter than its diff:
```python
import functools
import math

import jax
import jax.numpy as jnp
from jax import lax
from jax.experimental import pallas as pl
from jax.experimental.pallas import tpu as pltpu
from jax.sharding import PartitionSpec as P

MESH = pl.DeviceIdType.MESH
F32, BF16 = jnp.float32, jnp.bfloat16
HEAD_DIM = 32
LN2 = math.log(2.0)
LOG2E = math.log2(math.e)
NEG = -1000000000.0 * LOG2E
NT = (((1,), (1,)), ((), ()))


def dot(a, b):
    return jnp.dot(a, b, preferred_element_type=F32)


def dot_nt(a, b):
    return lax.dot_general(a, b, NT, preferred_element_type=F32)


def eye(n):
    rows = lax.broadcasted_iota(jnp.int32, (n, n), 0)
    cols = lax.broadcasted_iota(jnp.int32, (n, n), 1)
    return rows == cols


def norm(u, axis):
    center = u - jnp.mean(u, axis=axis, keepdims=True)
    spread = jnp.mean(center * center, axis=axis, keepdims=True)
    return center * lax.rsqrt(spread + 1e-05)


def kernel(
    x_h, type_h, mask_h, adj_h, ori_h, ttab_h, atab_h, otab_h, wqkv_h, wfilm_h,
    weo_h, wno_h, wnu_h, wnd_h, weu_h, wed_h, ng1_h, ng2_h, eg1_h, eg2_h,
    node_v, edge_v,
    type_s, mask_s,
    x_v, adj_v, ori_v, ttab_v, atab_v, otab_v, wqkv_v, wfilm_v,
    weo_v, wno_v, wnu_v, wnd_v, weu_v, wed_v, ng1_v, ng2_v, eg1_v, eg2_v,
    send, xq, xk, stat, rstat,
    t40, ft32, ftab, t40t, codes, onehot, film, score, e0, yrow,
    q_v, k_v, v_v, km_v, weut, g1c, g2c, u_s, e_s, h_s,
    in_sem, sendq, recvq, sendk, recvk, sends, recvs,
):
    gr, gc = lax.axis_index("gr"), lax.axis_index("gc")
    n_gr, n_gc = 4, 8

    barrier = pltpu.get_barrier_semaphore()
    home = lax.div(gc, 2)
    source = home == gr

    @pl.when(jnp.logical_not(source))
    def _():
        pl.semaphore_signal(barrier, inc=1, device_id={"gr": home}, device_id_type=MESH)

    for t in range(1, n_gc):
        pl.semaphore_signal(
            barrier, inc=1, device_id={"gc": lax.rem(gc + t, n_gc)}, device_id_type=MESH
        )
    pairs = [
        (x_h, x_v), (ttab_h, ttab_v), (adj_h, adj_v), (ori_h, ori_v),
        (atab_h, atab_v), (otab_h, otab_v), (wfilm_h, wfilm_v), (wqkv_h, wqkv_v),
        (weo_h, weo_v), (weu_h, weu_v), (wed_h, wed_v), (eg1_h, eg1_v), (eg2_h, eg2_v),
        (wno_h, wno_v), (wnu_h, wnu_v), (wnd_h, wnd_v), (ng1_h, ng1_v), (ng2_h, ng2_v),
        (type_h, type_s), (mask_h, mask_s),
    ]
    loads = [pltpu.make_async_copy(a, b, in_sem.at[i]) for i, (a, b) in enumerate(pairs)]
    for i in [18, 19] + list(range(18)):
        loads[i].start()

    for i in (18, 19, 0, 1):
        loads[i].wait()
    row_id = lax.broadcasted_iota(jnp.int32, (16, 256), 0)
    embedded = jnp.zeros((16, 256), F32)
    valid = jnp.zeros((16, 128), F32)
    for r in range(16):
        line = ttab_v[pl.ds(type_s[r], 1), :]
        embedded = jnp.where(row_id == r, line, embedded)
        valid = jnp.where(row_id[:, :128] == r, mask_s[r].astype(F32), valid)
    send[:, :256] = (x_v[...].astype(F32) + embedded).astype(BF16)
    send[:, 256:] = valid.astype(BF16)
    xq[pl.ds(gc, 1)] = send[...][None]

    def q_copy(peer, slot, index):
        return pltpu.make_async_remote_copy(
            src_ref=send, dst_ref=xq.at[slot], send_sem=sendq.at[index],
            recv_sem=recvq.at[slot], device_id={"gc": peer}, device_id_type=MESH,
        )

    def k_copy(peer, slot, index):
        return pltpu.make_async_remote_copy(
            src_ref=xq.at[4 * lax.rem(gc, 2) + slot], dst_ref=xk.at[slot], send_sem=sendk.at[index],
            recv_sem=recvk.at[slot], device_id={"gr": peer}, device_id_type=MESH,
        )

    @pl.when(source)
    def _():
        pl.semaphore_wait(barrier, n_gc - 1 + n_gr - 1)

    @pl.when(jnp.logical_not(source))
    def _():
        pl.semaphore_wait(barrier, n_gc - 1)

    q_sent = [q_copy(lax.rem(gc + t, n_gc), gc, t - 1) for t in (4, 3, 5, 2, 6, 1, 7)]
    for copy in q_sent:
        copy.start()
    for t in range(1, n_gc):
        @pl.when(source)
        def _():
            q_copy(gc, lax.rem(gc + t, n_gc), 0).wait_recv()

    @pl.when(source)
    def _():
        for t in (2, 1, 3):
            for slot in range(4):
                k_copy(lax.rem(gr + t, n_gr), slot, 3 * slot + t - 1).start()

    loads[4].wait()
    loads[5].wait()
    loads[6].wait()
    t40[...] = jnp.zeros_like(t40)
    ft32[...] = jnp.zeros_like(ft32)
    for a in range(5):
        t40[8 * a : 8 * a + 8, :32] = atab_v[a : a + 1, :] + otab_v[...]
    table = t40[...].astype(BF16)
    values = dot(table[:40, :32], wfilm_v[...])
    lane = lax.broadcasted_iota(jnp.int32, (40, 512), 1)
    values = values + jnp.where(lane < 256, 1.0, 0.0)
    values = values * LOG2E
    high = values.astype(BF16).astype(F32)
    middle = (values - high).astype(BF16).astype(F32)
    ft32[0:40] = high
    ft32[40:80] = middle
    ft32[80:120] = values - high - middle
    ftab[...] = ft32[...].astype(BF16)
    t40t[...] = t40[...].T[:32].astype(BF16)

    loads[2].wait()
    loads[3].wait()
    code = (adj_v[...] * 8 + ori_v[...]).astype(F32)
    code_t = jnp.concatenate([code, code], axis=0).T
    for b in range(8):
        codes[b] = pltpu.roll(code_t, (128 - 8 * b) % 128, 1)
    lane = lax.broadcasted_iota(jnp.int32, (128, 128), 1)
    label = jnp.where(lane < 40, lane, jnp.where(lane < 80, lane - 40, lane - 80))
    label = jnp.where(lane < 120, label, -1).astype(F32)

    for t in range(1, n_gc):
        @pl.when(jnp.logical_not(source))
        def _():
            q_copy(gc, lax.rem(gc + t, n_gc), 0).wait_recv()

    loads[7].wait()
    nodes_q = xq[...].reshape(128, 384)
    q = dot(nodes_q[:, :256], wqkv_v[:, :256]).astype(BF16)
    q_v[...] = q.astype(F32) * (1.0 / math.sqrt(HEAD_DIM))
    row_mask = nodes_q[:, 256:].astype(F32).T[0:1, :]

    def film_block(b, carry):
        block = codes[b]
        for r in range(8):
            hit = jnp.broadcast_to(block[:, r : r + 1], (128, 128)) == label
            onehot[128 * r : 128 * r + 128] = jnp.where(hit, 1.0, 0.0).astype(BF16)
        hot = onehot[...]
        film[pl.ds(b * 8, 8), :, :256] = dot(hot, ftab[:, :256]).reshape(8, 128, 256) * q_v[...][None]
        film[pl.ds(b * 8, 8), :, 256:] = dot(hot, ftab[:, 256:]).reshape(8, 128, 256)
        e0[:, pl.ds(pl.multiple_of(b * 1024, 1024), 1024)] = dot_nt(t40t[...], hot)
        return carry

    lax.fori_loop(0, 8, film_block, 0)

    for i in range(8, 13):
        loads[i].wait()
    weut[...] = weu_v[...].astype(F32).T.astype(BF16)
    for g_ref, c_ref in ((eg1_v, g1c), (eg2_v, g2c)):
        spread = jnp.where(eye(32), jnp.broadcast_to(g_ref[...], (32, 32)), 0.0)
        c_ref[...] = jnp.broadcast_to(jnp.sum(spread, axis=1, keepdims=True), (32, 128))

    @pl.when(jnp.logical_not(source))
    def _():
        for t in range(4):
            k_copy(gr, t, 0).wait_recv()

    @pl.when(source)
    def _():
        xk[...] = xq[pl.ds(4 * lax.rem(gc, 2), 4)]

    nodes_k = xk[...].reshape(64, 384)
    kv = dot(nodes_k[:, :256], wqkv_v[:, 256:]).astype(BF16).astype(F32)
    k_v[...] = kv[:, :256]
    v_v[...] = kv[:, 256:]
    km_v[...] = nodes_k[:, 256:].astype(F32)

    def s_copy(owner, slot, index):
        return pltpu.make_async_remote_copy(
            src_ref=stat.at[owner], dst_ref=rstat.at[slot], send_sem=sends.at[index],
            recv_sem=recvs.at[slot], device_id={"gc": owner}, device_id_type=MESH,
        )

    def owner_of(t):
        h = lax.div(t, 2)
        chip = lax.rem(lax.div(gc, 2) + 2 + h - lax.div(h, 2) * (2 * h - 1), 4)
        return 2 * chip + lax.rem(gc + t + 1, 2)

    def attend(t, carry):
        owner = owner_of(t)
        first = pl.multiple_of(owner * 16, 16)

        peak = jnp.full((16, 256), -3e38, F32)
        for j in range(64):
            live = jnp.broadcast_to(km_v[j : j + 1, :], (16, 128)) > 0
            live = jnp.concatenate([live, live], axis=1)
            k = jnp.broadcast_to(k_v[j : j + 1, :], (16, 256))
            s = k * film[j, pl.ds(first, 16), :256] + film[j, pl.ds(first, 16), 256:]
            s = jnp.where(live, s, NEG)
            score[j, pl.ds(first, 16), :] = s
            peak = jnp.maximum(peak, s)
        total = jnp.zeros((16, 256), F32)
        weighted = jnp.zeros((16, 256), F32)
        for j in range(64):
            v = jnp.broadcast_to(v_v[j : j + 1, :], (16, 256))
            p = jnp.exp2(score[j, pl.ds(first, 16), :] - peak)
            total = total + p
            weighted = weighted + p * v
        stat[owner, 0] = peak
        stat[owner, 1] = total
        stat[owner, 2] = weighted

        @pl.when(t >= 1)
        def _():
            s_copy(owner_of(t - 1), gc, t - 1).start()

        return carry

    lax.fori_loop(0, n_gc, attend, 0)

    gain1, gain2 = g1c[...], g2c[...]

    def message_stage(n):
        sb = (score[2 * n : 2 * n + 2].reshape(256, 256) * LN2).astype(BF16)
        u_s[n % 4] = e0[:, 256 * n : 256 * n + 256] + dot_nt(weo_v[...], sb)

    def norm_stage(n):
        for r in range(2):
            cols = slice(128 * r, 128 * r + 128)
            e_s[n % 8, :, cols] = (norm(u_s[n % 4, :, cols], 0) * gain1).astype(BF16)

    def up_stage(n):
        h_s[n % 4] = jnp.maximum(dot(weut[...], e_s[n % 8]).astype(BF16), 0.0)

    def down_stage(n):
        u = e_s[n % 8].astype(F32) + dot(wed_v[...], h_s[n % 4])
        for r in range(2):
            y = norm(u[:, 128 * r : 128 * r + 128], 0) * gain2
            yrow[(n // 8) % 2, pl.ds(2 * (n % 8) + r, 32, stride=16), :] = y
        if n % 8 == 7:
            at = 2 * n - 14
            keep = km_v[at : at + 16, :] * row_mask
            edge_v[:, at : at + 16, :] = (
                yrow[(n // 8) % 2].reshape(32, 16, 128) * keep[None]
            ).astype(BF16)

    for n in range(35):
        for lag, stage in enumerate((message_stage, norm_stage, up_stage, down_stage)):
            if 0 <= n - lag < 32:
                stage(n - lag)

    for i in range(13, 18):
        loads[i].wait()
    rstat[pl.ds(gc, 1)] = stat[pl.ds(gc, 1)]
    for t in range(1, n_gc):
        s_copy(gc, lax.rem(gc + t, n_gc), 0).wait_recv()
    peak = rstat[0, 0]
    for s in range(1, n_gc):
        peak = jnp.maximum(peak, rstat[s, 0])
    total = jnp.zeros((16, 256), F32)
    weighted = jnp.zeros((16, 256), F32)
    for s in range(n_gc):
        factor = jnp.exp2(rstat[s, 0] - peak)
        total = total + rstat[s, 1] * factor
        weighted = weighted + rstat[s, 2] * factor
    attn = (weighted / total).astype(BF16)
    own = send[...].astype(F32)
    n1 = (norm(own[:, :256] + dot(attn, wno_v[...]), 1) * ng1_v[...]).astype(BF16)
    hid = jnp.maximum(dot(n1, wnu_v[...]), 0.0).astype(BF16)
    n2 = norm(n1.astype(F32) + dot(hid, wnd_v[...]), 1) * ng2_v[...]
    node_v[...] = (n2 * jnp.concatenate([own[:, 256:]] * 2, axis=1)).astype(BF16)
    for copy in q_sent:
        copy.wait_send()

    @pl.when(source)
    def _():
        for t in range(12):
            k_copy(gr, 0, t).wait_send()

    for t in range(n_gc - 1):
        s_copy(gc, gc, t).wait_send()


def store(node_i, edge_i, node_o, edge_o, sem):
    copies = [
        pltpu.make_async_copy(edge_i, edge_o, sem.at[0]),
        pltpu.make_async_copy(node_i, node_o, sem.at[1]),
    ]
    for copy in copies:
        copy.start()
    for copy in copies:
        copy.wait()


def body(*args):
    (x_in, node_type, node_mask, adj, ori, ttab, atab, otab, wqkv, wfilm,
     weo, wno, wnu, wnd, weu, wed, ng1, ng2, eg1, eg2) = args
    args = (x_in, node_type, node_mask, adj, ori, ttab, atab, otab, wqkv, wfilm,
            weo.T, wno, wnu, wnd, weu, wed.T, ng1[None], ng2[None], eg1[None], eg2[None])
    anyspace = pl.BlockSpec(memory_space=pl.ANY)
    vmem = pl.BlockSpec(memory_space=pltpu.VMEM)
    hbm = pl.BlockSpec(memory_space=pltpu.HBM)
    V = pltpu.VMEM
    D = pltpu.SemaphoreType.DMA
    loaded = [args[0]] + list(args[3:])
    node, edge = pl.pallas_call(
        kernel,
        out_shape=(
            jax.ShapeDtypeStruct((16, 256), BF16),
            jax.ShapeDtypeStruct((32, 64, 128), BF16),
        ),
        in_specs=[hbm] * 20,
        out_specs=(vmem, vmem),
        scratch_shapes=[pltpu.SMEM((16,), jnp.int32)] * 2 + [V(a.shape, a.dtype) for a in loaded] + [
            V((16, 384), BF16),
            V((8, 16, 384), BF16),
            V((4, 16, 384), BF16),
            V((8, 3, 16, 256), F32),
            V((8, 3, 16, 256), F32),
            V((128, 128), F32),
            V((128, 512), F32),
            V((128, 512), BF16),
            V((32, 128), BF16),
            V((8, 128, 128), F32),
            V((1024, 128), BF16),
            V((64, 128, 512), F32),
            V((64, 128, 256), F32),
            V((32, 8192), F32),
            V((2, 512, 128), F32),
            V((128, 256), F32),
            V((64, 256), F32),
            V((64, 256), F32),
            V((64, 128), F32),
            V((128, 32), BF16),
            V((32, 128), F32),
            V((32, 128), F32),
            V((4, 32, 256), F32),
            V((8, 32, 256), BF16),
            V((4, 128, 256), BF16),
            D((20,)), D((7,)), D((8,)), D((12,)), D((4,)), D((7,)), D((8,)),
        ],
        compiler_params=pltpu.CompilerParams(
            collective_id=0, has_side_effects=True, vmem_limit_bytes=40 * 1024 * 1024
        ),
    )(*[pltpu.with_memory_space_constraint(a, pltpu.HBM) for a in args])
    return pl.pallas_call(
        store,
        out_shape=(
            jax.ShapeDtypeStruct((16, 256), BF16),
            jax.ShapeDtypeStruct((32, 64, 128), BF16),
        ),
        in_specs=[anyspace, anyspace],
        out_specs=(hbm, hbm),
        scratch_shapes=[D((2,))],
        compiler_params=pltpu.CompilerParams(vmem_limit_bytes=4 * 1024 * 1024),
    )(node, edge)


def solution(mesh):
    nodes = P(("graph", "gr", "gc"))
    rows = P(("graph", "gr", "gc"), None)
    pair = P(("graph", "gc"), "gr")
    return jax.shard_map(
        body,
        mesh=mesh,
        in_specs=(rows, nodes, nodes, pair, pair) + (P(),) * 15,
        out_specs=(rows, P(None, ("graph", "gc"), "gr")),
        check_vma=False,
    )
```

time: 36.8 us -> 29.8 us (0.81)
  local copies, waits for them, and re-layouts: 5.31 us -> 0 us
  Pallas kernels: 30.4 us -> 29 us
    unnamed x6 -> x0, local copies, waits for them, and re-layouts: 5.31 us -> none
    pallas_call x1, Pallas kernels: 30.4 us -> 28.2 us  [body(): pl.pallas_call(kernel, out_shape=(jax.ShapeDtypeStruct((16, 256), BF16),...]
    pallas_call x0 -> x1, Pallas kernels: none -> 0.81 us  [body(): pl.pallas_call(store, out_shape=(jax.ShapeDtypeStruct((16, 256), BF16), j...]
where the time goes in v2:
time: 29.8 us; the launch traced here: 29.6 us
  Pallas kernels  29 us (97%)
  between operations  0.65 us (2%)
    pallas_call x1, Pallas kernels, body(): pl.pallas_call(kernel, out_shape=(jax.ShapeDtypeStruct((16, 256), BF16),...  28.2 us
    pallas_call x1, Pallas kernels, body(): pl.pallas_call(store, out_shape=(jax.ShapeDtypeStruct((16, 256), BF16), j...  0.81 us

profile of v2, /device:TPU:1, one launch (start us, length us, event | category | flops | bytes accessed | tf_op | source)
XLA Modules:
  0.0 29.6 jit_solution(11459409941771421612)
XLA Ops:
  0.6 28.2 %shard_map.203 = (bf16[16,256]{1,0:T(8,128)(2,1)S(1)}, bf16[32,64,128]{2,1,0:T(8,128)(2,1)S(1)}) custom-call(bf16[16,256]{1,0:T(8,128)(2,1)} %x_h.1, s32[16]{0:T(128)} %type_h.1, s32[16]{0:T(128)} %mask_h.1, s32[64,128]{1,0:T(8,128)} %adj_h.1, s32[64,128]{1,0:T(8,128)} %ori_h.1, f32[8,256]{1,0:T(8,128)} %ttab_h.1, f32[5,32]{1,0:T(8,128)} %atab_h.1, ...), custom_call_target="tpu_custom_call" | custom-call | tf_op jit(solution)/shard_map/pallas_call | solution.py:329
  28.8 0.8 %shard_map.204 = (bf16[16,256]{1,0:T(8,128)(2,1)}, bf16[32,64,128]{2,1,0:T(8,128)(2,1)}) custom-call(bf16[16,256]{1,0:T(8,128)(2,1)S(1)} %get-tuple-element.4.node_i, bf16[32,64,128]{2,1,0:T(8,128)(2,1)S(1)} %get-tuple-element.5.edge_i), custom_call_target="tpu_custom_call" | custom-call | tf_op jit(solution)/shard_map/pallas_call | solution.py:369

commit v3 on v2

--- a/solution.py
+++ b/solution.py
@@ -229,9 +229,8 @@
             p = jnp.exp2(score[j, pl.ds(first, 16), :] - peak)
             total = total + p
             weighted = weighted + p * v
-        stat[owner, 0] = peak
-        stat[owner, 1] = total
-        stat[owner, 2] = weighted
+        stat[owner, 0] = peak + jnp.log(total) * LOG2E
+        stat[owner, 1] = weighted / total
 
         @pl.when(t >= 1)
         def _():
@@ -244,32 +243,40 @@
     gain1, gain2 = g1c[...], g2c[...]
 
     def message_stage(n):
-        sb = (score[2 * n : 2 * n + 2].reshape(256, 256) * LN2).astype(BF16)
-        u_s[n % 4] = e0[:, 256 * n : 256 * n + 256] + dot_nt(weo_v[...], sb)
+        for h in range(2):
+            m = 2 * n + h
+            sb = (score[2 * m : 2 * m + 2].reshape(256, 256) * LN2).astype(BF16)
+            u_s[m % 4] = e0[:, 256 * m : 256 * m + 256] + dot_nt(weo_v[...], sb)
 
     def norm_stage(n):
-        for r in range(2):
-            cols = slice(128 * r, 128 * r + 128)
-            e_s[n % 8, :, cols] = (norm(u_s[n % 4, :, cols], 0) * gain1).astype(BF16)
+        for h in range(2):
+            m = 2 * n + h
+            for r in range(2):
+                cols = slice(128 * r, 128 * r + 128)
+                e_s[m % 8, :, cols] = (norm(u_s[m % 4, :, cols], 0) * gain1).astype(BF16)
 
     def up_stage(n):
-        h_s[n % 4] = jnp.maximum(dot(weut[...], e_s[n % 8]).astype(BF16), 0.0)
+        for h in range(2):
+            m = 2 * n + h
+            h_s[m % 4] = jnp.maximum(dot(weut[...], e_s[m % 8]).astype(BF16), 0.0)
 
     def down_stage(n):
-        u = e_s[n % 8].astype(F32) + dot(wed_v[...], h_s[n % 4])
-        for r in range(2):
-            y = norm(u[:, 128 * r : 128 * r + 128], 0) * gain2
-            yrow[(n // 8) % 2, pl.ds(2 * (n % 8) + r, 32, stride=16), :] = y
-        if n % 8 == 7:
-            at = 2 * n - 14
+        for h in range(2):
+            m = 2 * n + h
+            u = e_s[m % 8].astype(F32) + dot(wed_v[...], h_s[m % 4])
+            for r in range(2):
+                y = norm(u[:, 128 * r : 128 * r + 128], 0) * gain2
+                yrow[(m // 8) % 2, pl.ds(2 * (m % 8) + r, 32, stride=16), :] = y
+        if n % 4 == 3:
+            at = 4 * n - 12
             keep = km_v[at : at + 16, :] * row_mask
             edge_v[:, at : at + 16, :] = (
-                yrow[(n // 8) % 2].reshape(32, 16, 128) * keep[None]
+                yrow[(n // 4) % 2].reshape(32, 16, 128) * keep[None]
             ).astype(BF16)
 
-    for n in range(35):
+    for n in range(19):
         for lag, stage in enumerate((message_stage, norm_stage, up_stage, down_stage)):
-            if 0 <= n - lag < 32:
+            if 0 <= n - lag < 16:
                 stage(n - lag)
 
     for i in range(13, 18):
@@ -284,8 +291,8 @@
     weighted = jnp.zeros((16, 256), F32)
     for s in range(n_gc):
         factor = jnp.exp2(rstat[s, 0] - peak)
-        total = total + rstat[s, 1] * factor
-        weighted = weighted + rstat[s, 2] * factor
+        total = total + factor
+        weighted = weighted + rstat[s, 1] * factor
     attn = (weighted / total).astype(BF16)
     own = send[...].astype(F32)
     n1 = (norm(own[:, :256] + dot(attn, wno_v[...]), 1) * ng1_v[...]).astype(BF16)
@@ -338,8 +345,8 @@
             V((16, 384), BF16),
             V((8, 16, 384), BF16),
             V((4, 16, 384), BF16),
-            V((8, 3, 16, 256), F32),
-            V((8, 3, 16, 256), F32),
+            V((8, 2, 16, 256), F32),
+            V((8, 2, 16, 256), F32),
             V((128, 128), F32),
             V((128, 512), F32),
             V((128, 512), BF16),

time: 29.8 us -> 29.2 us (0.980)
  Pallas kernels: 29 us -> 28.4 us
    pallas_call x1, Pallas kernels: 28.2 us -> 27.6 us  [body(): pl.pallas_call(kernel, out_shape=(jax.ShapeDtypeStruct((16, 256), BF16),...]
where the time goes in v3:
time: 29.2 us; the launch traced here: 29.1 us
  Pallas kernels  28.4 us (97%)
  between operations  0.65 us (2%)
    pallas_call x1, Pallas kernels, body(): pl.pallas_call(kernel, out_shape=(jax.ShapeDtypeStruct((16, 256), BF16),...  27.6 us
    pallas_call x1, Pallas kernels, body(): pl.pallas_call(store, out_shape=(jax.ShapeDtypeStruct((16, 256), BF16), j...  0.81 us

profile of v3, /device:TPU:1, one launch (start us, length us, event | category | flops | bytes accessed | tf_op | source)
XLA Modules:
  0.0 29.1 jit_solution(13998794578660158406)
XLA Ops:
  0.6 27.6 %shard_map.203 = (bf16[16,256]{1,0:T(8,128)(2,1)S(1)}, bf16[32,64,128]{2,1,0:T(8,128)(2,1)S(1)}) custom-call(bf16[16,256]{1,0:T(8,128)(2,1)} %x_h.1, s32[16]{0:T(128)} %type_h.1, s32[16]{0:T(128)} %mask_h.1, s32[64,128]{1,0:T(8,128)} %adj_h.1, s32[64,128]{1,0:T(8,128)} %ori_h.1, f32[8,256]{1,0:T(8,128)} %ttab_h.1, f32[5,32]{1,0:T(8,128)} %atab_h.1, ...), custom_call_target="tpu_custom_call" | custom-call | tf_op jit(solution)/shard_map/pallas_call | solution.py:336
  28.3 0.8 %shard_map.204 = (bf16[16,256]{1,0:T(8,128)(2,1)}, bf16[32,64,128]{2,1,0:T(8,128)(2,1)}) custom-call(bf16[16,256]{1,0:T(8,128)(2,1)S(1)} %get-tuple-element.4.node_i, bf16[32,64,128]{2,1,0:T(8,128)(2,1)S(1)} %get-tuple-element.5.edge_i), custom_call_target="tpu_custom_call" | custom-call | tf_op jit(solution)/shard_map/pallas_call | solution.py:376

commit v4 on v3

--- a/solution.py
+++ b/solution.py
@@ -152,25 +152,13 @@
     label = jnp.where(lane < 40, lane, jnp.where(lane < 80, lane - 40, lane - 80))
     label = jnp.where(lane < 120, label, -1).astype(F32)
 
-    for t in range(1, n_gc):
-        @pl.when(jnp.logical_not(source))
-        def _():
-            q_copy(gc, lax.rem(gc + t, n_gc), 0).wait_recv()
-
-    loads[7].wait()
-    nodes_q = xq[...].reshape(128, 384)
-    q = dot(nodes_q[:, :256], wqkv_v[:, :256]).astype(BF16)
-    q_v[...] = q.astype(F32) * (1.0 / math.sqrt(HEAD_DIM))
-    row_mask = nodes_q[:, 256:].astype(F32).T[0:1, :]
-
     def film_block(b, carry):
         block = codes[b]
         for r in range(8):
             hit = jnp.broadcast_to(block[:, r : r + 1], (128, 128)) == label
             onehot[128 * r : 128 * r + 128] = jnp.where(hit, 1.0, 0.0).astype(BF16)
         hot = onehot[...]
-        film[pl.ds(b * 8, 8), :, :256] = dot(hot, ftab[:, :256]).reshape(8, 128, 256) * q_v[...][None]
-        film[pl.ds(b * 8, 8), :, 256:] = dot(hot, ftab[:, 256:]).reshape(8, 128, 256)
+        film[pl.ds(b * 8, 8)] = dot(hot, ftab[...]).reshape(8, 128, 512)
         e0[:, pl.ds(pl.multiple_of(b * 1024, 1024), 1024)] = dot_nt(t40t[...], hot)
         return carry
 
@@ -182,6 +170,26 @@
     for g_ref, c_ref in ((eg1_v, g1c), (eg2_v, g2c)):
         spread = jnp.where(eye(32), jnp.broadcast_to(g_ref[...], (32, 32)), 0.0)
         c_ref[...] = jnp.broadcast_to(jnp.sum(spread, axis=1, keepdims=True), (32, 128))
+
+    for t in range(1, n_gc):
+        @pl.when(jnp.logical_not(source))
+        def _():
+            q_copy(gc, lax.rem(gc + t, n_gc), 0).wait_recv()
+
+    loads[7].wait()
+    nodes_q = xq[...].reshape(128, 384)
+    q = dot(nodes_q[:, :256], wqkv_v[:, :256]).astype(BF16)
+    q_v[...] = q.astype(F32) * (1.0 / math.sqrt(HEAD_DIM))
+    row_mask = nodes_q[:, 256:].astype(F32).T[0:1, :]
+
+    def scale_block(b, carry):
+        rows = pl.ds(pl.multiple_of(b * 16, 16), 16)
+        qs = q_v[rows, :]
+        for j in range(64):
+            film[j, rows, :256] = film[j, rows, :256] * qs
+        return carry
+
+    lax.fori_loop(0, 8, scale_block, 0)
 
     @pl.when(jnp.logical_not(source))
     def _():

time: 29.2 us -> 29.2 us (level)
  no operation moved by 1% of the time
where the time goes in v4:
time: 29.2 us; the launch traced here: 29.1 us
  Pallas kernels  28.4 us (97%)
  between operations  0.65 us (2%)
    pallas_call x1, Pallas kernels, body(): pl.pallas_call(kernel, out_shape=(jax.ShapeDtypeStruct((16, 256), BF16),...  27.6 us
    pallas_call x1, Pallas kernels, body(): pl.pallas_call(store, out_shape=(jax.ShapeDtypeStruct((16, 256), BF16), j...  0.81 us

profile of v4, /device:TPU:1, one launch (start us, length us, event | category | flops | bytes accessed | tf_op | source)
XLA Modules:
  0.0 29.1 jit_solution(15323701438026555062)
XLA Ops:
  0.6 27.6 %shard_map.203 = (bf16[16,256]{1,0:T(8,128)(2,1)S(1)}, bf16[32,64,128]{2,1,0:T(8,128)(2,1)S(1)}) custom-call(bf16[16,256]{1,0:T(8,128)(2,1)} %x_h.1, s32[16]{0:T(128)} %type_h.1, s32[16]{0:T(128)} %mask_h.1, s32[64,128]{1,0:T(8,128)} %adj_h.1, s32[64,128]{1,0:T(8,128)} %ori_h.1, f32[8,256]{1,0:T(8,128)} %ttab_h.1, f32[5,32]{1,0:T(8,128)} %atab_h.1, ...), custom_call_target="tpu_custom_call" | custom-call | tf_op jit(solution)/shard_map/pallas_call | solution.py:344
  28.3 0.8 %shard_map.204 = (bf16[16,256]{1,0:T(8,128)(2,1)}, bf16[32,64,128]{2,1,0:T(8,128)(2,1)}) custom-call(bf16[16,256]{1,0:T(8,128)(2,1)S(1)} %get-tuple-element.4.node_i, bf16[32,64,128]{2,1,0:T(8,128)(2,1)S(1)} %get-tuple-element.5.edge_i), custom_call_target="tpu_custom_call" | custom-call | tf_op jit(solution)/shard_map/pallas_call | solution.py:384
